TPU v7x, 256 devices: a whole 4x4x8 slice. The times are simulated.
256 devices in a mesh: row: 16 (over x_hi, z), col: 16 (over y, x_lo, core).
Axes of the slice: x: 4 (x_hi: 2, x_lo: 2; x = x_hi * 2 + x_lo), y: 4, z: 8, core: 2. Of those that a mesh axis runs over, the one named last changes fastest.
Arguments:
- charges: bfloat16 [2097152], P(('row', 'col')), may hold values from -6 to 6
- panel_order: int32 [2097152], P(('row', 'col')), may hold values from 0 to 8191, as said below
- patch_anchor: int32 [3, 32768], P(None, ('row', 'col')), may hold values from 0 to 252, as said below
- project: bfloat16 [32768, 4096], P(('row', 'col')), may hold values from -0.75 to 0.75
- interpolate: bfloat16 [32768, 4096], P(('row', 'col')), may hold values from -0.75 to 0.75
- kernel_spectrum: float32 [512, 512, 512], P('row', 'col'), may hold values from 0.5 to 8
- near_pairs: int32 [2, 131072], P(None, ('row', 'col')), may hold values from 0 to 32767, as said below
- near_blocks: bfloat16 [131072, 4096], P(('row', 'col')), may hold values from -0.75 to 0.75
Outputs:
- potential: float32 [2097152], P(('row', 'col'))
Inputs may be any that keep to these rules, and one draw needn't show every extreme that they name: `panel_order`: the entries of each aligned run of 8192 slots (one device's slots) are a permutation of 0 to 8191. `patch_anchor`: block b lies on device d = b // 128 at row index r = d // 16 and col index c = d % 16; its first coordinate lies in r * 16 to (r + 1) * 16 - 1, its second in c * 16 to (c + 1) * 16 - 1, and all three coordinates are at most 252. `near_pairs`: the pairs on a device have that device's blocks as targets, each block exactly 4 times; each source block lies on the same device or on one whose row and col indices each differ by at most one.
All inputs are finite; a program needn't handle non-finite values.
Results may differ from a plain program's by a relative error of at most 0.0025.
Values may be sent and summed in bfloat16 or wider, within the bound.
A program may use at most 128 MiB of HBM per device.

v0:
```python
import math

import jax
import jax.numpy as jnp
import numpy as np
from jax import lax
from jax.experimental import pallas as pl
from jax.experimental.pallas import tpu as pltpu
from jax.sharding import PartitionSpec as P

G = 256
P_SIZE = 512
BLK = 64
PTS = 64
N = 16
OWN = 256
EXT = 368
CH = 4
F32 = jnp.float32
BF16 = jnp.bfloat16
LANES = 128
ROWS = 64
PICK = 384
I32 = jnp.int32
NEIGHBOURS = [(a, b) for a in (-1, 0, 1) for b in (-1, 0, 1) if (a, b) != (0, 0)]


def tables():
    first = np.arange(G)[:, None]
    second = np.arange(P_SIZE)[None, :]
    phase = (first * second % P_SIZE).astype(np.float64) * (2.0 * math.pi / P_SIZE)
    table = (np.cos(phase) + np.sin(phase)) / math.sqrt(P_SIZE)
    high = table.astype(BF16)
    low = (table - high.astype(np.float64)).astype(BF16)
    forward = np.stack([high, low])
    backward = np.stack([high.T, low.T])
    swap = np.zeros((P_SIZE, P_SIZE), np.float32)
    x, f = np.meshgrid(np.arange(16), np.arange(32), indexing="ij")
    swap[x * 32 + f, f * 16 + x] = 1.0
    swap = swap.astype(BF16)
    into = np.stack([swap[:, 128 * k : 128 * k + 128] for k in range(CH)])
    back = np.stack([swap.T[128 * k : 128 * k + 128, :] for k in range(CH)])
    return forward, backward, into, back


def transposed_groups(parts, lanes):
    count = len(parts)
    group = 128 // count
    distance = count // 2
    parts = list(parts)
    while distance:
        shift = distance * group
        upper = (lanes // shift) % 2 == 1
        for q in range(count):
            if q & distance:
                continue
            a, b = parts[q], parts[q + distance]
            parts[q] = jnp.where(upper, pltpu.roll(b, shift, 1), a)
            parts[q + distance] = jnp.where(upper, b, pltpu.roll(a, 128 - shift, 1))
        distance //= 2
    return parts


def dot(a, b):
    return jnp.dot(a, b, preferred_element_type=F32)


def iota(shape, axis):
    return lax.broadcasted_iota(I32, shape, axis)


def halves(x):
    high = x.astype(BF16)
    return high, (x - high.astype(F32)).astype(BF16)


def one_hot(mask):
    return jnp.where(mask, 1.0, 0.0).astype(BF16)


def looked_up(table, places):
    return jnp.take_along_axis(table, places, axis=1)


def permuted(table, order):
    upper, lower = order >> 7, order & 127
    out = jnp.zeros((ROWS, LANES), F32)
    for k in range(ROWS):
        line = jnp.broadcast_to(table[k : k + 1, :], (ROWS, LANES))
        out = jnp.where(upper == k, looked_up(line, lower), out)
    return out


def column(line):
    eye = iota((LANES, LANES), 0) == iota((LANES, LANES), 1)
    spread = jnp.where(eye, jnp.broadcast_to(line.astype(F32), (LANES, LANES)), 0.0)
    return dot(spread.astype(BF16), jnp.ones((LANES, LANES), BF16))


def block_sums(mats, start, vec):
    both = jnp.concatenate([vec, vec], axis=1)

    def step(n, total):
        cols = pl.ds(pl.multiple_of(256 * n, 256), 256)
        high, low = halves(mats[pl.ds(start, LANES), cols].astype(F32) * both)
        group = one_hot((iota((256, BLK), 0) >> 6) + 4 * n == iota((256, BLK), 1))
        return total + dot(jnp.concatenate([high, low], axis=0), group)

    total = lax.fori_loop(0, 16, step, jnp.zeros((256, BLK), F32))
    return total[:LANES] + total[LANES:]


def solve_kernel(
    charges, order, anchor, pairs, project_hbm, interp_hbm, near_hbm, k_hbm, fwd, bwd, into, back,
    out_ref,
    pv, iv, nv, ext, qd, codes, picks, zrow, slots, terms, field_ref, inverse,
    kv, halo_y, halo_x, halo_c, g0, s1, sb1, r1, sb2, r2, sb3, r3, sb4, r4, acc,
    fld, sy, sx, sc, ry, rx, rc, nb,
    in_sem, k_sem, hs_sem, hr_sem, ns_sem, nr_sem, s1_sem, r1_sem, s2_sem, r2_sem, s3_sem, r3_sem,
    s4_sem, r4_sem, os_sem, or_sem,
):
    row = lax.axis_index("row")
    col = lax.axis_index("col")
    mesh_id = pl.DeviceIdType.MESH

    def at(a, b):
        return (lax.rem(row + a + N, N), lax.rem(col + b + N, N))

    barrier = pltpu.get_barrier_semaphore()

    def greet(k, _):
        pl.semaphore_signal(barrier, inc=1, device_id=at(k, 0), device_id_type=mesh_id)
        pl.semaphore_signal(barrier, inc=1, device_id=at(0, k), device_id_type=mesh_id)
        return 0

    lax.fori_loop(1, N, greet, 0)
    for a in (-1, 1):
        for b in (-1, 1):
            pl.semaphore_signal(barrier, inc=1, device_id=at(a, b), device_id_type=mesh_id)
    p_copy = pltpu.make_async_copy(project_hbm, pv, in_sem.at[0])
    i_copy = pltpu.make_async_copy(interp_hbm, iv, in_sem.at[1])
    n_copy = pltpu.make_async_copy(near_hbm, nv, in_sem.at[2])
    p_copy.start()
    k_copies = [
        pltpu.make_async_copy(k_hbm.at[:, pl.ds(128 * h, 128)], kv.at[h], k_sem.at[h])
        for h in range(CH)
    ]
    for copy in k_copies:
        copy.start()
    n_copy.start()
    i_copy.start()

    permutation = order[...]
    q_slots = permuted(charges[...].astype(F32), permutation)
    block_of = iota((LANES, ROWS), 0) >> 1
    q_rows = dot(one_hot(block_of == iota((LANES, ROWS), 1)), q_slots.astype(BF16))
    odd = (iota((LANES, LANES), 0) & 1) == 1
    right = iota((LANES, LANES), 1) >= BLK
    q_both = jnp.where(odd == right, q_rows, pltpu.roll(q_rows, BLK, 1))
    qd[...] = q_both.astype(BF16)
    p_copy.wait()
    patch = block_sums(pv, 0, q_both)
    patch_high, patch_low = halves(patch)
    x0 = anchor[0:1, :] - 16 * row
    y0 = anchor[1:2, :] - 16 * col
    z0 = anchor[2:3, :]
    sheet = jnp.concatenate(
        [patch_high, patch_low] + [column(v).astype(BF16) for v in (z0, x0, y0)], axis=1
    )
    corner_rows = jnp.concatenate(
        [x0.astype(F32), y0.astype(F32), jnp.zeros((14, LANES), F32)], axis=0
    ).astype(BF16)
    ext[...] = jnp.zeros_like(ext)

    def code_of(x, y):
        inside = x * 16 + y
        past_y = 256 + (y - 16) * 16 + x
        past_x = 304 + (x - 16) * 16 + y
        corner = 352 + (x - 16) * 4 + (y - 16)
        return jnp.where(
            x < 16, jnp.where(y < 16, inside, past_y), jnp.where(y < 16, past_x, corner)
        )

    def scatter(n, _):
        rows = dot(one_hot((iota((256, LANES), 0) >> 4) + 16 * n == iota((256, LANES), 1)), sheet)
        point = iota((256, LANES), 0) & 15
        lane = iota((256, LANES), 1)
        z = rows[:, 128:256].astype(I32)
        x = rows[:, 256:384].astype(I32) + (point >> 2)
        y = rows[:, 384:512].astype(I32) + (point & 3)
        zrow[n] = z
        codes[n] = code_of(x, y)
        values = rows[:, 0:128] + pltpu.roll(rows[:, 0:128], BLK, 1)
        pieces = []
        for h in range(2):
            off = lane + 128 * h - z
            seen = (off >= 0) & (off < 4)
            places = 4 * point + jnp.clip(off, 0, 3)
            pieces += halves(jnp.where(seen, looked_up(values, places), 0.0))
        lines = dot(
            corner_rows,
            one_hot((iota((LANES, 256), 1) >> 4) + 16 * n == iota((LANES, 256), 0)),
        ).astype(I32)
        at_point = iota((1, 256), 1) & 15
        code = code_of(lines[0:1] + (at_point >> 2), lines[1:2] + (at_point & 3))
        pick = one_hot(iota((EXT, 256), 0) == code)
        added = dot(pick, jnp.concatenate(pieces, axis=1))
        ext[0] += added[:, 0:128] + added[:, 128:256]
        ext[1] += added[:, 256:384] + added[:, 384:512]
        return 0

    lax.fori_loop(0, 8, scatter, 0)
    pl.semaphore_wait(barrier, 2 * (N - 1) + 4)

    def remote(src, dst, send, recv, who):
        return pltpu.make_async_remote_copy(
            src_ref=src, dst_ref=dst, send_sem=send, recv_sem=recv,
            device_id=who, device_id_type=mesh_id,
        )

    def drained(ref, sem):
        pltpu.make_async_copy(ref, ref, sem).wait()

    halo_copies = [
        remote(ext.at[:, pl.ds(256, 48)], halo_y, hs_sem.at[0], hr_sem.at[0], at(0, 1)),
        remote(ext.at[:, pl.ds(304, 48)], halo_x, hs_sem.at[1], hr_sem.at[1], at(1, 0)),
        remote(ext.at[:, pl.ds(352, 16)], halo_c, hs_sem.at[2], hr_sem.at[2], at(1, 1)),
    ]
    for copy in halo_copies:
        copy.start()
    near_copies = []
    for k, (a, b) in enumerate(NEIGHBOURS):
        slot = NEIGHBOURS.index((-a, -b))
        near_copies.append(remote(qd, nb.at[slot], ns_sem.at[k], nr_sem.at[slot], at(a, b)))
    for copy in near_copies:
        copy.start()
    g0[...] = ext[:, :OWN, :]
    source = pairs[1:2, :]
    place = source >> 7
    slot = ((place >> 4) - row + 1) * 3 + ((place & 15) - col + 1)
    slot = jnp.where(slot == 4, 8, jnp.where(slot > 4, slot - 1, slot))
    for t in range(4):
        cut = slice(128 * t, 128 * t + 128)
        slots[t, 0:1] = slot[:, cut]
        slots[t, 1:2] = (source & 127)[:, cut]
    for copy in halo_copies:
        copy.wait()
    for h in range(2):
        for k in range(3):
            g0[h, pl.ds(k, 16, stride=16), :] += halo_y[h, 16 * k : 16 * k + 16, :]
        g0[h, 0:48, :] += halo_x[h]
        for k in range(3):
            g0[h, 16 * k : 16 * k + 4, :] += halo_c[h, 4 * k : 4 * k + 4, :]

    lanes = lax.broadcasted_iota(jnp.int32, (1, 128), 1)

    def exchange(src, dst, me, send, recv, along):
        def one(k, _):
            to = lax.rem(me + k, N)
            who = (row, to) if along == "col" else (to, col)
            remote(src.at[to], dst.at[me], send, recv, who).start()
            return 0

        lax.fori_loop(1, N, one, 0)
        dst[me] = src[me]

    grid = jnp.concatenate([g0[0], g0[1]], axis=1)
    high = grid.astype(BF16)
    low = (grid - high.astype(F32)).astype(BF16)
    s1[...] = (dot(high, fwd[0]) + dot(high, fwd[1]) + dot(low, fwd[0])).reshape(4, 4, 16, 512)
    for k in range(4):
        parts = [s1[:, q, :, 128 * k : 128 * k + 128].reshape(64, 128) for q in range(4)]
        for q, part in enumerate(transposed_groups(parts, lanes)):
            sb1[4 * k + q] = part.reshape(4, 16, 128).astype(BF16)
    exchange(sb1, r1, col, s1_sem, r1_sem, "col")
    drained(r1.at[pl.ds(0, N - 1)], r1_sem)

    def second(k, _):
        lines = dot(r1[:, 0].reshape(256, 128), into[k, 0:128])
        for j in range(1, 4):
            lines += dot(r1[:, j].reshape(256, 128), into[k, 128 * j : 128 * j + 128])
        lines = lines.astype(BF16)
        out = dot(bwd[0], lines) + dot(bwd[1], lines)
        sb2[k] = out.astype(BF16).reshape(N, 32, 128)
        exchange(sb2.at[k], r2.at[k], row, s2_sem.at[k], r2_sem.at[k], "row")
        return 0

    lax.fori_loop(0, CH, second, 0)
    for copy in k_copies:
        copy.wait()

    for copy in near_copies:
        copy.wait()
    n_copy.wait()

    def near_part(t):
        slot_rows = column(slots[t, 0:1]).astype(I32)
        place_rows = column(slots[t, 1:2]).astype(I32)
        lane = iota((LANES, LANES), 1)
        picked = jnp.zeros((LANES, LANES), F32)
        for s in range(9):
            table = qd[...] if s == 8 else nb[s]
            picked += dot(one_hot((slot_rows == s) & (place_rows == lane)), table)
        terms[t] = block_sums(nv, pl.multiple_of(128 * t, 128), picked)

    def first(k, _):
        near_part(k)
        drained(r2.at[k, pl.ds(0, N - 1)], r2_sem.at[k])
        halves = []
        for h in range(2):
            parts = [r2[k, 8 * h + q].astype(F32) for q in range(8)]
            halves.append(jnp.concatenate(transposed_groups(parts, lanes), axis=0).astype(BF16))
        lines = jnp.concatenate(halves, axis=1)
        spec = dot(lines, fwd[0]) + dot(lines, fwd[1])
        cols = []
        for h in range(CH):
            weights = jnp.concatenate(
                [kv[h, pl.ds(8 * k + q, 32, stride=32), :] for q in range(8)], axis=0
            )
            cols.append((spec[:, 128 * h : 128 * h + 128] * weights).astype(BF16))
        weighted = jnp.concatenate(cols, axis=1)
        field = dot(weighted, bwd[0]) + dot(weighted, bwd[1])
        for h in range(2):
            parts = [field[32 * q : 32 * q + 32, 128 * h : 128 * h + 128] for q in range(8)]
            for q, part in enumerate(transposed_groups(parts, lanes)):
                sb3[k, 8 * h + q] = part.astype(BF16)
        exchange(sb3.at[k], r3.at[k], row, s3_sem.at[k], r3_sem.at[k], "row")
        return 0

    lax.fori_loop(0, CH, first, 0)
    near = jnp.zeros((LANES, BLK), F32)
    for t in range(4):
        target = pairs[0:1, 128 * t : 128 * t + 128] - 128 * (row * N + col)
        hot = one_hot(iota((LANES, LANES), 0) == target)
        for part in halves(terms[t]):
            near += dot(hot, part)
    terms[0] = near
    inverse[...] = jnp.zeros_like(inverse)

    def inverted(k, total):
        lines = order[pl.ds(pl.multiple_of(8 * k, 8), 8), :]
        for j in range(8):
            line = lines[j : j + 1, :]
            at_row = iota((ROWS, LANES), 0) == (line >> 7)
            both = jnp.concatenate(
                [
                    jnp.where(at_row, iota((ROWS, LANES), 1).astype(F32), 0.0),
                    jnp.where(at_row, (8 * k + j).astype(F32), 0.0),
                ],
                axis=0,
            ).astype(BF16)
            hot = one_hot(iota((LANES, LANES), 0) == (line & 127))
            total += lax.dot_general(
                both, hot, (((1,), (1,)), ((), ())), preferred_element_type=F32
            )
        return total

    def picking(n):
        for j in range(3):
            lane = iota((256, LANES), 1) + 128 * j
            picks[n, :, 128 * j : 128 * j + 128] = one_hot(codes[n] == lane)

    acc[...] = jnp.zeros_like(acc)

    def second_back(k, _):
        inverse[...] += inverted(2 * k, inverted(2 * k + 1, jnp.zeros((LANES, LANES), F32)))
        picking(2 * k)
        picking(2 * k + 1)
        drained(r3.at[k, pl.ds(0, N - 1)], r3_sem.at[k])
        lines = r3[k].reshape(512, 128)
        part = (dot(fwd[0], lines) + dot(fwd[1], lines)).astype(BF16)
        acc[...] += dot(part, back[k])
        return 0

    lax.fori_loop(0, CH, second_back, 0)
    for j in range(4):
        sb4[:, j] = acc[:, 128 * j : 128 * j + 128].astype(BF16).reshape(16, 16, 128)
    exchange(sb4, r4, col, s4_sem, r4_sem, "col")
    drained(r4.at[pl.ds(0, N - 1)], r4_sem)
    for k in range(4):
        parts = [r4[4 * k + q].astype(F32).reshape(64, 128) for q in range(4)]
        for q, part in enumerate(transposed_groups(parts, lanes)):
            s1[:, q, :, 128 * k : 128 * k + 128] = part.reshape(4, 16, 128)
    lines = s1[...].reshape(256, 512).astype(BF16)
    field = dot(lines, bwd[0]) + dot(lines, bwd[1])
    for h in range(2):
        fld[h] = field[:, 128 * h : 128 * h + 128]
    sx[...] = field[0:48].astype(BF16)
    for h in range(2):
        sy[:, 128 * h : 128 * h + 128] = jnp.concatenate(
            [fld[h, pl.ds(k, 16, stride=16), :] for k in range(3)], axis=0
        ).astype(BF16)
        sc[:, 128 * h : 128 * h + 128] = jnp.concatenate(
            [fld[h, 16 * k : 16 * k + 4, :] for k in range(4)], axis=0
        ).astype(BF16)
    out_copies = [
        remote(sy, ry, os_sem.at[0], or_sem.at[0], at(0, -1)),
        remote(sx, rx, os_sem.at[1], or_sem.at[1], at(-1, 0)),
        remote(sc, rc, os_sem.at[2], or_sem.at[2], at(-1, -1)),
    ]
    for copy in out_copies:
        copy.start()
    field_ref[0:OWN] = field.astype(BF16)
    field_ref[EXT:PICK] = jnp.zeros((PICK - EXT, G), BF16)
    drained(sb1.at[pl.ds(0, N - 1)], s1_sem)
    drained(sb4.at[pl.ds(0, N - 1)], s4_sem)
    for k in range(CH):
        drained(sb2.at[k, pl.ds(0, N - 1)], s2_sem.at[k])
        drained(sb3.at[k, pl.ds(0, N - 1)], s3_sem.at[k])
    for copy in out_copies:
        copy.wait()
    field_ref[256:304] = ry[...]
    field_ref[304:352] = rx[...]
    field_ref[352:368] = rc[...]
    i_copy.wait()

    def gathered(n, _):
        taken = dot(picks[n], field_ref[...])
        point = iota((256, LANES), 0) & 15
        lane = iota((256, LANES), 1)
        z = zrow[n] + (lane & 3)
        value = jnp.where(
            z < 128,
            looked_up(taken[:, 0:128], jnp.minimum(z, 127)),
            looked_up(taken[:, 128:256], jnp.maximum(z - 128, 0)),
        )
        value = jnp.where(((lane >> 2) & 15) == point, value, 0.0)
        fld[0, pl.ds(pl.multiple_of(16 * n, 16), 16), :] = jnp.sum(
            value.reshape(16, 16, LANES), axis=1
        )
        return 0

    lax.fori_loop(0, 8, gathered, 0)
    total = block_sums(iv, 0, fld[0, 0:LANES, :]) + terms[0]
    total = jnp.concatenate([total, total], axis=1)
    total = jnp.where(odd == right, total, 0.0)
    gather_rows = one_hot(iota((ROWS, LANES), 0) == (iota((ROWS, LANES), 1) >> 1))
    by_slot = sum(dot(gather_rows, part) for part in halves(total))
    back_order = inverse[...].astype(I32)
    out_ref[...] = permuted(by_slot, back_order[ROWS:] * 128 + back_order[:ROWS])


def solve(charges, order, anchor, pairs, project, interpolate, near_blocks, kernel_spectrum):
    forward, backward, into, back = tables()
    vmem = pl.BlockSpec(memory_space=pltpu.VMEM)
    hbm = pl.BlockSpec(memory_space=pl.ANY)
    dma = pltpu.SemaphoreType.DMA
    return pl.pallas_call(
        solve_kernel,
        out_shape=jax.ShapeDtypeStruct((ROWS, LANES), F32),
        in_specs=[vmem] * 4 + [hbm] * 4 + [vmem] * 4,
        out_specs=vmem,
        scratch_shapes=[
            pltpu.VMEM((128, 4096), BF16),
            pltpu.VMEM((128, 4096), BF16),
            pltpu.VMEM((512, 4096), BF16),
            pltpu.VMEM((2, EXT, 128), F32),
            pltpu.VMEM((LANES, LANES), BF16),
            pltpu.VMEM((8, 256, LANES), I32),
            pltpu.VMEM((8, 256, PICK), BF16),
            pltpu.VMEM((8, 256, LANES), I32),
            pltpu.VMEM((4, 8, LANES), I32),
            pltpu.VMEM((4, LANES, BLK), F32),
            pltpu.VMEM((PICK, G), BF16),
            pltpu.VMEM((LANES, LANES), F32),
            pltpu.VMEM((CH, 1024, 128), F32),
            pltpu.VMEM((2, 48, 128), F32),
            pltpu.VMEM((2, 48, 128), F32),
            pltpu.VMEM((2, 16, 128), F32),
            pltpu.VMEM((2, OWN, 128), F32),
            pltpu.VMEM((4, 4, 16, 512), F32),
            pltpu.VMEM((N, 4, 16, 128), BF16),
            pltpu.VMEM((N, 4, 16, 128), BF16),
            pltpu.VMEM((CH, N, 32, 128), BF16),
            pltpu.VMEM((CH, N, 32, 128), BF16),
            pltpu.VMEM((CH, N, 32, 128), BF16),
            pltpu.VMEM((CH, N, 32, 128), BF16),
            pltpu.VMEM((N, 4, 16, 128), BF16),
            pltpu.VMEM((N, 4, 16, 128), BF16),
            pltpu.VMEM((OWN, P_SIZE), F32),
            pltpu.VMEM((2, OWN, 128), F32),
            pltpu.VMEM((48, G), BF16),
            pltpu.VMEM((48, G), BF16),
            pltpu.VMEM((16, G), BF16),
            pltpu.VMEM((48, G), BF16),
            pltpu.VMEM((48, G), BF16),
            pltpu.VMEM((16, G), BF16),
            pltpu.VMEM((8, LANES, LANES), BF16),
            dma((3,)),
            dma((CH,)),
            dma((3,)),
            dma((3,)),
            dma((8,)),
            dma((8,)),
            dma(()),
            dma(()),
            dma((CH,)),
            dma((CH,)),
            dma((CH,)),
            dma((CH,)),
            dma(()),
            dma(()),
            dma((3,)),
            dma((3,)),
        ],
        compiler_params=pltpu.CompilerParams(
            collective_id=0, has_side_effects=True, vmem_limit_bytes=48 << 20
        ),
    )(
        charges.reshape(ROWS, LANES),
        order.reshape(ROWS, LANES),
        anchor,
        pairs,
        project,
        interpolate,
        near_blocks,
        kernel_spectrum.reshape(1024, P_SIZE),
        jnp.asarray(forward),
        jnp.asarray(backward),
        jnp.asarray(into),
        jnp.asarray(back),
    )


def body(
    charges,
    panel_order,
    patch_anchor,
    project,
    interpolate,
    kernel_spectrum,
    near_pairs,
    near_blocks,
):
    out = solve(
        charges, panel_order, patch_anchor, near_pairs, project, interpolate, near_blocks,
        kernel_spectrum,
    )
    return out.reshape(ROWS * LANES)


def solution(mesh):
    placed = (
        P(("row", "col")),
        P(("row", "col")),
        P(None, ("row", "col")),
        P(("row", "col"), None),
        P(("row", "col"), None),
        P("row", "col", None),
        P(None, ("row", "col")),
        P(("row", "col"), None),
    )
    return jax.shard_map(
        body, mesh=mesh, in_specs=placed, out_specs=P(("row", "col")), check_vma=False
    )
```

profile of v0, /device:TPU:1, one launch (start us, length us, event | category | flops | bytes accessed | tf_op | source)
XLA Modules:
  0.0 89.3 jit_solution(5429182351508913926)
XLA Ops:
  0.0 0.0 copy-start
  0.0 1.2 %copy-done = bf16[128,4096]{1,0:T(8,128)(2,1)S(1)} copy-done((bf16[128,4096]{1,0:T(8,128)(2,1)S(1)}, bf16[128,4096]{1,0:T(8,128)(2,1)}, u32[]{:S(2)}) %copy-start) | copy-done | bytes 1048600
  1.2 0.0 copy-start.1
  1.2 1.2 %copy-done.1 = bf16[128,4096]{1,0:T(8,128)(2,1)S(1)} copy-done((bf16[128,4096]{1,0:T(8,128)(2,1)S(1)}, bf16[128,4096]{1,0:T(8,128)(2,1)}, u32[]{:S(2)}) %copy-start.1) | copy-done | bytes 1048600
  2.5 0.0 copy-start.2
  2.5 1.0 %copy-done.2 = bf16[4,128,512]{2,1,0:T(8,128)(2,1)S(1)} copy-done((bf16[4,128,512]{2,1,0:T(8,128)(2,1)S(1)}, bf16[4,128,512]{2,1,0:T(8,128)(2,1)}, u32[]{:S(2)}) %copy-start.2) | copy-done | bytes 524312
  3.5 0.0 copy-start.3
  3.5 1.0 %copy-done.3 = bf16[4,512,128]{2,1,0:T(8,128)(2,1)S(1)} copy-done((bf16[4,512,128]{2,1,0:T(8,128)(2,1)S(1)}, bf16[4,512,128]{2,1,0:T(8,128)(2,1)}, u32[]{:S(2)}) %copy-start.3) | copy-done | bytes 524312
  4.5 0.0 copy-start.4
  4.5 1.0 %copy-done.4 = bf16[2,512,256]{2,1,0:T(8,128)(2,1)S(1)} copy-done((bf16[2,512,256]{2,1,0:T(8,128)(2,1)S(1)}, bf16[2,512,256]{2,1,0:T(8,128)(2,1)}, u32[]{:S(2)}) %copy-start.4) | copy-done | bytes 524312
  5.6 0.0 copy-start.5
  5.6 1.0 %copy-done.5 = bf16[2,256,512]{2,1,0:T(8,128)(2,1)S(1)} copy-done((bf16[2,256,512]{2,1,0:T(8,128)(2,1)S(1)}, bf16[2,256,512]{2,1,0:T(8,128)(2,1)}, u32[]{:S(2)}) %copy-start.5) | copy-done | bytes 524312
  6.6 0.0 copy-start.6
  6.6 0.8 copy-done.6
  7.4 0.0 copy-start.7
  7.4 0.7 copy-done.7
  8.1 0.0 copy-start.8
  8.1 0.7 copy-done.8
  8.8 0.0 copy-start.9
  8.8 0.7 copy-done.9
  9.5 79.3 %shard_map.118 = f32[64,128]{1,0:T(8,128)S(1)} custom-call(bf16[64,128]{1,0:T(8,128)(2,1)S(1)} %bitcast.6, s32[64,128]{1,0:T(8,128)S(1)} %bitcast.5, s32[3,128]{1,0:T(4,128)S(1)} %copy-done.9, s32[2,512]{1,0:T(2,128)S(1)} %copy-done.8, bf16[128,4096]{1,0:T(8,128)(2,1)S(1)} %copy-done, bf16[128,4096]{1,0:T(8,128)(2,1)S(1)} %copy-done.1, ...), custom_call_target="tpu_custom_call" | custom-call | tf_op jit(solution)/shard_map/pallas_call | solution.py:448
  88.7 0.6 copy.14
Async XLA Ops:
  0.0 1.2 %copy-start = (bf16[128,4096]{1,0:T(8,128)(2,1)S(1)}, bf16[128,4096]{1,0:T(8,128)(2,1)}, u32[]{:S(2)}) copy-start(bf16[128,4096]{1,0:T(8,128)(2,1)} %project_hbm.1) | copy-start | bytes 3145732
  1.2 1.2 %copy-start.1 = (bf16[128,4096]{1,0:T(8,128)(2,1)S(1)}, bf16[128,4096]{1,0:T(8,128)(2,1)}, u32[]{:S(2)}) copy-start(bf16[128,4096]{1,0:T(8,128)(2,1)} %interp_hbm.1) | copy-start | bytes 3145732
  2.5 1.0 %copy-start.2 = (bf16[4,128,512]{2,1,0:T(8,128)(2,1)S(1)}, bf16[4,128,512]{2,1,0:T(8,128)(2,1)}, u32[]{:S(2)}) copy-start(bf16[4,128,512]{2,1,0:T(8,128)(2,1)} %constant.11.clone.back) | copy-start | bytes 1572868
  3.5 1.0 %copy-start.3 = (bf16[4,512,128]{2,1,0:T(8,128)(2,1)S(1)}, bf16[4,512,128]{2,1,0:T(8,128)(2,1)}, u32[]{:S(2)}) copy-start(bf16[4,512,128]{2,1,0:T(8,128)(2,1)} %constant.10.clone.into) | copy-start | bytes 1572868
  4.5 1.0 %copy-start.4 = (bf16[2,512,256]{2,1,0:T(8,128)(2,1)S(1)}, bf16[2,512,256]{2,1,0:T(8,128)(2,1)}, u32[]{:S(2)}) copy-start(bf16[2,512,256]{2,1,0:T(8,128)(2,1)} %constant.9.clone.bwd) | copy-start | bytes 1572868
  5.6 1.0 %copy-start.5 = (bf16[2,256,512]{2,1,0:T(8,128)(2,1)S(1)}, bf16[2,256,512]{2,1,0:T(8,128)(2,1)}, u32[]{:S(2)}) copy-start(bf16[2,256,512]{2,1,0:T(8,128)(2,1)} %constant.8.clone.fwd) | copy-start | bytes 1572868
  6.6 0.8 copy-start.6
  7.4 0.7 copy-start.7
  8.1 0.7 copy-start.8
  8.8 0.7 copy-start.9
where the time goes:
time: 89.9 us; the launch traced here: 89.3 us
  Pallas kernels  79.3 us (88%)
  local copies, waits for them, and re-layouts  10.1 us (11%)
    pallas_call x1, Pallas kernels, solve(): pl.pallas_call(solve_kernel, out_shape=jax.ShapeDtypeStruct((ROWS, LANES)...  79.3 us
    unnamed x21, local copies, waits for them, and re-layouts  10.1 us

commit v1 on v0

--- a/solution.py
+++ b/solution.py
@@ -97,22 +97,28 @@
     return dot(spread.astype(BF16), jnp.ones((LANES, LANES), BF16))
 
 
-def block_sums(mats, start, vec):
-    both = jnp.concatenate([vec, vec], axis=1)
-
-    def step(n, total):
-        cols = pl.ds(pl.multiple_of(256 * n, 256), 256)
-        high, low = halves(mats[pl.ds(start, LANES), cols].astype(F32) * both)
-        group = one_hot((iota((256, BLK), 0) >> 6) + 4 * n == iota((256, BLK), 1))
-        return total + dot(jnp.concatenate([high, low], axis=0), group)
-
-    total = lax.fori_loop(0, 16, step, jnp.zeros((256, BLK), F32))
+def block_sums(mats, start, vec, group):
+    high, low = [], []
+    for n in range(32):
+        part = mats[pl.ds(start, LANES), 128 * n : 128 * n + 128].astype(F32) * vec
+        one, two = halves(part)
+        high.append(one)
+        low.append(two)
+    total = jnp.zeros((256, LANES), F32)
+    for q in range(4):
+        cut = slice(8 * q, 8 * q + 8)
+        both = jnp.concatenate(
+            [jnp.concatenate(high[cut], axis=1), jnp.concatenate(low[cut], axis=1)], axis=0
+        )
+        total += dot(both, group[1024 * q : 1024 * q + 1024])
     return total[:LANES] + total[LANES:]
 
 
 def solve_kernel(
-    charges, order, anchor, pairs, project_hbm, interp_hbm, near_hbm, k_hbm, fwd, bwd, into, back,
+    charges_hbm, order_hbm, anchor_hbm, pairs_hbm, project_hbm, interp_hbm, near_hbm, k_hbm,
+    fwd_hbm, bwd_hbm, into_hbm, back_hbm,
     out_ref,
+    charges, order, anchor, pairs, fwd, bwd, into, back, group, spots, placed, pick,
     pv, iv, nv, ext, qd, codes, picks, zrow, slots, terms, field_ref, inverse,
     kv, halo_y, halo_x, halo_c, g0, s1, sb1, r1, sb2, r2, sb3, r3, sb4, r4, acc,
     fld, sy, sx, sc, ry, rx, rc, nb,
@@ -137,10 +143,24 @@
     for a in (-1, 1):
         for b in (-1, 1):
             pl.semaphore_signal(barrier, inc=1, device_id=at(a, b), device_id_type=mesh_id)
+    small = [
+        pltpu.make_async_copy(src, dst, in_sem.at[3 + n])
+        for n, (src, dst) in enumerate(
+            [
+                (order_hbm, order), (charges_hbm, charges), (anchor_hbm, anchor),
+                (pairs_hbm, pairs), (fwd_hbm, fwd), (bwd_hbm, bwd), (into_hbm, into),
+                (back_hbm, back),
+            ]
+        )
+    ]
+    for copy in small[:4]:
+        copy.start()
     p_copy = pltpu.make_async_copy(project_hbm, pv, in_sem.at[0])
     i_copy = pltpu.make_async_copy(interp_hbm, iv, in_sem.at[1])
     n_copy = pltpu.make_async_copy(near_hbm, nv, in_sem.at[2])
     p_copy.start()
+    for copy in small[4:]:
+        copy.start()
     k_copies = [
         pltpu.make_async_copy(k_hbm.at[:, pl.ds(128 * h, 128)], kv.at[h], k_sem.at[h])
         for h in range(CH)
@@ -150,6 +170,16 @@
     n_copy.start()
     i_copy.start()
 
+    def grouped(n, _):
+        rows = pl.ds(pl.multiple_of(512 * n, 512), 512)
+        group[rows] = one_hot(
+            (iota((512, LANES), 0) >> 6) + 8 * n == (iota((512, LANES), 1) & (BLK - 1))
+        )
+        return 0
+
+    lax.fori_loop(0, 8, grouped, 0)
+    for copy in small[:4]:
+        copy.wait()
     permutation = order[...]
     q_slots = permuted(charges[...].astype(F32), permutation)
     block_of = iota((LANES, ROWS), 0) >> 1
@@ -159,8 +189,8 @@
     q_both = jnp.where(odd == right, q_rows, pltpu.roll(q_rows, BLK, 1))
     qd[...] = q_both.astype(BF16)
     p_copy.wait()
-    patch = block_sums(pv, 0, q_both)
-    patch_high, patch_low = halves(patch)
+    patch = block_sums(pv, 0, q_both, group)
+    patch_high, patch_low = halves(patch[:, :BLK])
     x0 = anchor[0:1, :] - 16 * row
     y0 = anchor[1:2, :] - 16 * col
     z0 = anchor[2:3, :]
@@ -170,8 +200,6 @@
     corner_rows = jnp.concatenate(
         [x0.astype(F32), y0.astype(F32), jnp.zeros((14, LANES), F32)], axis=0
     ).astype(BF16)
-    ext[...] = jnp.zeros_like(ext)
-
     def code_of(x, y):
         inside = x * 16 + y
         past_y = 256 + (y - 16) * 16 + x
@@ -180,6 +208,12 @@
         return jnp.where(
             x < 16, jnp.where(y < 16, inside, past_y), jnp.where(y < 16, past_x, corner)
         )
+
+    lines = dot(
+        corner_rows, one_hot((iota((LANES, 2048), 1) >> 4) == iota((LANES, 2048), 0))
+    ).astype(I32)
+    at_point = iota((1, 2048), 1) & 15
+    spots[0:1] = code_of(lines[0:1] + (at_point >> 2), lines[1:2] + (at_point & 3))
 
     def scatter(n, _):
         rows = dot(one_hot((iota((256, LANES), 0) >> 4) + 16 * n == iota((256, LANES), 1)), sheet)
@@ -197,19 +231,17 @@
             seen = (off >= 0) & (off < 4)
             places = 4 * point + jnp.clip(off, 0, 3)
             pieces += halves(jnp.where(seen, looked_up(values, places), 0.0))
-        lines = dot(
-            corner_rows,
-            one_hot((iota((LANES, 256), 1) >> 4) + 16 * n == iota((LANES, 256), 0)),
-        ).astype(I32)
-        at_point = iota((1, 256), 1) & 15
-        code = code_of(lines[0:1] + (at_point >> 2), lines[1:2] + (at_point & 3))
-        pick = one_hot(iota((EXT, 256), 0) == code)
-        added = dot(pick, jnp.concatenate(pieces, axis=1))
-        ext[0] += added[:, 0:128] + added[:, 128:256]
-        ext[1] += added[:, 256:384] + added[:, 384:512]
-        return 0
-
-    lax.fori_loop(0, 8, scatter, 0)
+        here = pl.ds(pl.multiple_of(256 * n, 256), 256)
+        placed[here] = jnp.concatenate(pieces, axis=1)
+        pick[:, here] = one_hot(iota((EXT, 256), 0) == spots[0:1, here])
+        return 0
+
+    lax.fori_loop(0, 8, scatter, 0, unroll=2)
+    added = dot(pick[...], placed[...])
+    ext[0] = added[:, 0:128] + added[:, 128:256]
+    ext[1] = added[:, 256:384] + added[:, 384:512]
+    for copy in small[4:]:
+        copy.wait()
     pl.semaphore_wait(barrier, 2 * (N - 1) + 4)
 
     def remote(src, dst, send, recv, who):
@@ -301,7 +333,7 @@
         for s in range(9):
             table = qd[...] if s == 8 else nb[s]
             picked += dot(one_hot((slot_rows == s) & (place_rows == lane)), table)
-        terms[t] = block_sums(nv, pl.multiple_of(128 * t, 128), picked)
+        terms[t] = block_sums(nv, pl.multiple_of(128 * t, 128), picked, group)
 
     def first(k, _):
         near_part(k)
@@ -328,7 +360,7 @@
         return 0
 
     lax.fori_loop(0, CH, first, 0)
-    near = jnp.zeros((LANES, BLK), F32)
+    near = jnp.zeros((LANES, LANES), F32)
     for t in range(4):
         target = pairs[0:1, 128 * t : 128 * t + 128] - 128 * (row * N + col)
         hot = one_hot(iota((LANES, LANES), 0) == target)
@@ -430,9 +462,8 @@
         )
         return 0
 
-    lax.fori_loop(0, 8, gathered, 0)
-    total = block_sums(iv, 0, fld[0, 0:LANES, :]) + terms[0]
-    total = jnp.concatenate([total, total], axis=1)
+    lax.fori_loop(0, 8, gathered, 0, unroll=2)
+    total = block_sums(iv, 0, fld[0, 0:LANES, :], group) + terms[0]
     total = jnp.where(odd == right, total, 0.0)
     gather_rows = one_hot(iota((ROWS, LANES), 0) == (iota((ROWS, LANES), 1) >> 1))
     by_slot = sum(dot(gather_rows, part) for part in halves(total))
@@ -448,9 +479,21 @@
     return pl.pallas_call(
         solve_kernel,
         out_shape=jax.ShapeDtypeStruct((ROWS, LANES), F32),
-        in_specs=[vmem] * 4 + [hbm] * 4 + [vmem] * 4,
+        in_specs=[hbm] * 12,
         out_specs=vmem,
         scratch_shapes=[
+            pltpu.VMEM((ROWS, LANES), BF16),
+            pltpu.VMEM((ROWS, LANES), I32),
+            pltpu.VMEM((3, LANES), I32),
+            pltpu.VMEM((2, 512), I32),
+            pltpu.VMEM((2, 256, 512), BF16),
+            pltpu.VMEM((2, 512, 256), BF16),
+            pltpu.VMEM((4, 512, 128), BF16),
+            pltpu.VMEM((4, 128, 512), BF16),
+            pltpu.VMEM((4096, LANES), BF16),
+            pltpu.VMEM((8, 2048), I32),
+            pltpu.VMEM((2048, 512), BF16),
+            pltpu.VMEM((EXT, 2048), BF16),
             pltpu.VMEM((128, 4096), BF16),
             pltpu.VMEM((128, 4096), BF16),
             pltpu.VMEM((512, 4096), BF16),
@@ -460,7 +503,7 @@
             pltpu.VMEM((8, 256, PICK), BF16),
             pltpu.VMEM((8, 256, LANES), I32),
             pltpu.VMEM((4, 8, LANES), I32),
-            pltpu.VMEM((4, LANES, BLK), F32),
+            pltpu.VMEM((4, LANES, LANES), F32),
             pltpu.VMEM((PICK, G), BF16),
             pltpu.VMEM((LANES, LANES), F32),
             pltpu.VMEM((CH, 1024, 128), F32),
@@ -486,7 +529,7 @@
             pltpu.VMEM((48, G), BF16),
             pltpu.VMEM((16, G), BF16),
             pltpu.VMEM((8, LANES, LANES), BF16),
-            dma((3,)),
+            dma((11,)),
             dma((CH,)),
             dma((3,)),
             dma((3,)),
@@ -504,7 +547,7 @@
             dma((3,)),
         ],
         compiler_params=pltpu.CompilerParams(
-            collective_id=0, has_side_effects=True, vmem_limit_bytes=48 << 20
+            collective_id=0, has_side_effects=True, vmem_limit_bytes=62 << 20
         ),
     )(
         charges.reshape(ROWS, LANES),

time: 89.9 us -> 69.5 us (0.77)
  Pallas kernels: 79.3 us -> 68 us
  local copies, waits for them, and re-layouts: 10.1 us -> 1.38 us
    pallas_call x1, Pallas kernels: 79.3 us -> 68 us  [solve(): pl.pallas_call(solve_kernel, out_shape=jax.ShapeDtypeStruct((ROWS, LANES)...]
    unnamed x21 -> x1, local copies, waits for them, and re-layouts: 10.1 us -> 1.38 us
where the time goes in v1:
time: 69.5 us; the launch traced here: 69.4 us
  Pallas kernels  68 us (98%)
  local copies, waits for them, and re-layouts  1.38 us (2%)
    pallas_call x1, Pallas kernels, solve(): pl.pallas_call(solve_kernel, out_shape=jax.ShapeDtypeStruct((ROWS, LANES)...  68 us

profile of v1, /device:TPU:1, one launch (start us, length us, event | category | flops | bytes accessed | tf_op | source)
XLA Modules:
  0.0 69.4 jit_solution(7280884940255228981)
XLA Ops:
  0.0 68.0 %shard_map.118 = f32[64,128]{1,0:T(8,128)} custom-call(bf16[64,128]{1,0:T(8,128)(2,1)} %bitcast.7, s32[64,128]{1,0:T(8,128)} %bitcast.6, s32[3,128]{1,0:T(4,128)} %anchor_hbm.1, s32[2,512]{1,0:T(2,128)} %pairs_hbm.1, bf16[128,4096]{1,0:T(8,128)(2,1)} %project_hbm.1, bf16[128,4096]{1,0:T(8,128)(2,1)} %interp_hbm.1, bf16[512,4096]{1,0:T(8,128)(2,1)} %near_hbm.1, ...), custom_call_target="tpu_custom_call" | custom-call | tf_op jit(solution)/shard_map/pallas_call | solution.py:479
  68.0 1.4 %copy.14 = f32[8192]{0:T(1024)} copy(f32[8192]{0:T(1024)} %bitcast.5) | data formatting | bytes 65536

commit v2 on v1

v2 whole, which is shorter than its diff:
```python
import math

import jax
import jax.numpy as jnp
import numpy as np
from jax import lax
from jax.experimental import pallas as pl
from jax.experimental.pallas import tpu as pltpu
from jax.sharding import PartitionSpec as P

G = 256
P_SIZE = 512
BLK = 64
PTS = 64
N = 16
TALL = 24
WIDE = 20
EXT = TALL * WIDE
CH = 2
F32 = jnp.float32
BF16 = jnp.bfloat16
LANES = 128
ROWS = 64
PICK = 512
I32 = jnp.int32
NEIGHBOURS = [(a, b) for a in (-1, 0, 1) for b in (-1, 0, 1) if (a, b) != (0, 0)]


def tables():
    first = np.arange(G)[:, None]
    second = np.arange(P_SIZE)[None, :]
    phase = (first * second % P_SIZE).astype(np.float64) * (2.0 * math.pi / P_SIZE)
    table = (np.cos(phase) + np.sin(phase)) / math.sqrt(P_SIZE)
    high = table.astype(BF16)
    low = (table - high.astype(np.float64)).astype(BF16)
    backward = np.stack([high.T, low.T])
    reach = np.zeros((N, TALL), np.int64) - 1
    for c in range(N):
        for y in range(19):
            if 16 * c + y < G:
                reach[c, y] = 16 * c + y
    reach = reach.reshape(N * TALL)
    keep = (reach >= 0)[:, None]
    padded = np.stack([np.where(keep, part[reach], 0).astype(BF16) for part in (high, low)])
    x, f = np.meshgrid(np.arange(16), np.arange(8), indexing="ij")
    near_x, near_f = np.meshgrid(np.arange(3), np.arange(8), indexing="ij")
    into = np.zeros((4, 256, 128), np.float32)
    for k in range(4):
        into[k, x * 8 + f, f * 16 + x] = 1.0
        into[k, 128 + near_x * 32 + 8 * k + near_f, near_f * 16 + near_x] = 1.0
    into = into.astype(BF16)
    back = np.transpose(into, (0, 2, 1)).copy()
    tall = padded.reshape(2, N, TALL, P_SIZE)
    return backward, padded.transpose(0, 2, 1).copy(), tall, into, back


def transposed_groups(parts, lanes):
    count = len(parts)
    group = 128 // count
    distance = count // 2
    parts = list(parts)
    while distance:
        shift = distance * group
        upper = (lanes // shift) % 2 == 1
        for q in range(count):
            if q & distance:
                continue
            a, b = parts[q], parts[q + distance]
            parts[q] = jnp.where(upper, pltpu.roll(b, shift, 1), a)
            parts[q + distance] = jnp.where(upper, b, pltpu.roll(a, 128 - shift, 1))
        distance //= 2
    return parts


def dot(a, b):
    return jnp.dot(a, b, preferred_element_type=F32)


def iota(shape, axis):
    return lax.broadcasted_iota(I32, shape, axis)


def halves(x):
    high = x.astype(BF16)
    return high, (x - high.astype(F32)).astype(BF16)


def one_hot(mask):
    return jnp.where(mask, 1.0, 0.0).astype(BF16)


def looked_up(table, places):
    return jnp.take_along_axis(table, places, axis=1)


def permuted(table, order):
    upper, lower = order >> 7, order & 127
    out = jnp.zeros((ROWS, LANES), F32)
    for k in range(ROWS):
        line = jnp.broadcast_to(table[k : k + 1, :], (ROWS, LANES))
        out = jnp.where(upper == k, looked_up(line, lower), out)
    return out


def column(line):
    eye = iota((LANES, LANES), 0) == iota((LANES, LANES), 1)
    spread = jnp.where(eye, jnp.broadcast_to(line.astype(F32), (LANES, LANES)), 0.0)
    return dot(spread.astype(BF16), jnp.ones((LANES, LANES), BF16))


def block_sums(mats, start, vec, group):
    high, low = [], []
    for n in range(32):
        part = mats[pl.ds(start, LANES), 128 * n : 128 * n + 128].astype(F32) * vec
        one, two = halves(part)
        high.append(one)
        low.append(two)
    total = jnp.zeros((256, LANES), F32)
    for q in range(4):
        cut = slice(8 * q, 8 * q + 8)
        both = jnp.concatenate(
            [jnp.concatenate(high[cut], axis=1), jnp.concatenate(low[cut], axis=1)], axis=0
        )
        total += dot(both, group[1024 * q : 1024 * q + 1024])
    return total[:LANES] + total[LANES:]


def solve_kernel(
    charges_hbm, order_hbm, anchor_hbm, pairs_hbm, project_hbm, interp_hbm, near_hbm, k_hbm,
    bwd_hbm, yfwd_hbm, ybwd_hbm, into_hbm, back_hbm,
    out_ref,
    charges, order, anchor, pairs, bwd, yfwd, ybwd, into, back, group, zline,
    pv, iv, nv, qd, cells, slots, terms, inverse,
    kv, s1, sb1, r1, hs1, hr1, sb2, r2, sb3, r3, sb4, r4, hs4, hr4, acc, nb,
    in_sem, k_sem, ns_sem, nr_sem, s1_sem, r1_sem, s2_sem, r2_sem, s3_sem, r3_sem,
    s4_sem, r4_sem, h_sem,
):
    row = lax.axis_index("row")
    col = lax.axis_index("col")
    mesh_id = pl.DeviceIdType.MESH

    def at(a, b):
        return (lax.rem(row + a + N, N), lax.rem(col + b + N, N))

    barrier = pltpu.get_barrier_semaphore()

    def greet(k, _):
        pl.semaphore_signal(barrier, inc=1, device_id=at(k, 0), device_id_type=mesh_id)
        pl.semaphore_signal(barrier, inc=1, device_id=at(0, k), device_id_type=mesh_id)
        return 0

    lax.fori_loop(1, N, greet, 0)

    def greet_beside(k, _):
        pl.semaphore_signal(barrier, inc=1, device_id=at(1, k), device_id_type=mesh_id)
        pl.semaphore_signal(barrier, inc=1, device_id=at(-1, k), device_id_type=mesh_id)
        return 0

    lax.fori_loop(1, N, greet_beside, 0)
    small = [
        pltpu.make_async_copy(src, dst, in_sem.at[3 + n])
        for n, (src, dst) in enumerate(
            [
                (order_hbm, order), (charges_hbm, charges), (anchor_hbm, anchor),
                (pairs_hbm, pairs), (bwd_hbm, bwd), (yfwd_hbm, yfwd),
                (ybwd_hbm, ybwd), (into_hbm, into), (back_hbm, back),
            ]
        )
    ]
    for copy in small[:4]:
        copy.start()
    p_copy = pltpu.make_async_copy(project_hbm, pv, in_sem.at[0])
    i_copy = pltpu.make_async_copy(interp_hbm, iv, in_sem.at[1])
    n_copy = pltpu.make_async_copy(near_hbm, nv, in_sem.at[2])
    p_copy.start()
    for copy in small[4:]:
        copy.start()
    k_copies = [
        pltpu.make_async_copy(k_hbm.at[:, pl.ds(128 * h, 128)], kv.at[h], k_sem.at[h])
        for h in range(4)
    ]
    for copy in k_copies:
        copy.start()
    n_copy.start()
    i_copy.start()

    def grouped(n, _):
        rows = pl.ds(pl.multiple_of(512 * n, 512), 512)
        group[rows] = one_hot(
            (iota((512, LANES), 0) >> 6) + 8 * n == (iota((512, LANES), 1) & (BLK - 1))
        )
        return 0

    lax.fori_loop(0, 8, grouped, 0)
    for copy in small[:4]:
        copy.wait()
    permutation = order[...]
    q_slots = permuted(charges[...].astype(F32), permutation)
    block_of = iota((LANES, ROWS), 0) >> 1
    q_rows = dot(one_hot(block_of == iota((LANES, ROWS), 1)), q_slots.astype(BF16))
    odd = (iota((LANES, LANES), 0) & 1) == 1
    right = iota((LANES, LANES), 1) >= BLK
    q_both = jnp.where(odd == right, q_rows, pltpu.roll(q_rows, BLK, 1))
    qd[...] = q_both.astype(BF16)
    p_copy.wait()
    patch = block_sums(pv, 0, q_both, group)
    for copy in small[4:]:
        copy.wait()
    x_rows = column(anchor[0:1, :] - 16 * row).astype(I32)
    y_rows = column(anchor[1:2, :] - 16 * col).astype(I32)
    z_rows = column(anchor[2:3, :]).astype(I32)
    corner = 16 * x_rows + 4 * y_rows
    lane = iota((LANES, LANES), 1)
    spot = (x_rows + (lane >> 4)) * TALL + y_rows + ((lane >> 2) & 3)
    cells[...] = jnp.where(lane < BLK, spot, 0)
    at_z = jnp.concatenate(
        [
            jnp.concatenate([one_hot(z_rows + l == lane + 128 * h) for h in range(2)], axis=1)
            for l in range(4)
        ],
        axis=0,
    )
    for n in range(2):
        zline[n] = dot(at_z, ybwd[n, :, 0:16].reshape(G, P_SIZE)).astype(BF16)
    seen, places = [], []
    for h in range(4):
        cell = iota((1, LANES), 1) + 128 * h
        cell_x = lax.div(cell, TALL)
        cell_y = cell - TALL * cell_x
        seen.append((((cell_x - x_rows) | (cell_y - y_rows)) >> 2) == 0)
        places.append((16 * cell_x + 4 * cell_y) - corner)
    weights = []
    for l in range(4):
        weights.append(
            jnp.concatenate(
                [
                    jnp.where(seen[h], looked_up(patch, (places[h] + l) & (LANES - 1)), 0.0)
                    for h in range(4)
                ],
                axis=1,
            )
        )
    high, low = halves(jnp.concatenate(weights, axis=0))

    def across(a, b):
        return lax.dot_general(a, b, (((0,), (0,)), ((), ())), preferred_element_type=F32)

    lanes = lax.broadcasted_iota(I32, (1, 128), 1)
    spread = across(high, zline[0]) + across(high, zline[1]) + across(low, zline[0])
    s1[...] = spread[0:EXT].reshape(WIDE, TALL, 512)
    for k in range(4):
        cols = slice(128 * k, 128 * k + 128)
        parts = [s1[q, :, cols] for q in range(16)]
        for q, part in enumerate(transposed_groups(parts, lanes)):
            j = q % 4
            sb1[j // 2, 4 * k + q // 4, j % 2] = part.astype(BF16)
        parts = [s1[16 + q, :, cols] for q in range(4)]
        for q, part in enumerate(transposed_groups(parts, lanes)):
            hs1[4 * k + q] = part.astype(BF16)
    pl.semaphore_wait(barrier, 4 * (N - 1))

    def remote(src, dst, send, recv, who):
        return pltpu.make_async_remote_copy(
            src_ref=src, dst_ref=dst, send_sem=send, recv_sem=recv,
            device_id=who, device_id_type=mesh_id,
        )

    def drained(ref, sem):
        pltpu.make_async_copy(ref, ref, sem).wait()

    def exchange(src, dst, me, send, recv, along):
        def one(k, _):
            to = lax.rem(me + k, N)
            who = (row, to) if along == "col" else (to, col)
            remote(src.at[to], dst.at[me], send, recv, who).start()
            return 0

        lax.fori_loop(1, N, one, 0)
        dst[me] = src[me]

    def exchange_beside(src, dst, send, recv, step):
        def one(k, _):
            to = lax.rem(col + k, N)
            who = (lax.rem(row + step + N, N), to)
            remote(src.at[to], dst.at[col], send, recv, who).start()
            return 0

        lax.fori_loop(0, N, one, 0)

    exchange(sb1.at[0], r1.at[0], col, s1_sem.at[0], r1_sem.at[0], "col")
    exchange_beside(hs1, hr1, h_sem.at[0], h_sem.at[1], 1)
    exchange(sb1.at[1], r1.at[1], col, s1_sem.at[1], r1_sem.at[1], "col")
    near_copies = []
    for k, (a, b) in enumerate(NEIGHBOURS):
        slot = NEIGHBOURS.index((-a, -b))
        near_copies.append(remote(qd, nb.at[slot], ns_sem.at[k], nr_sem.at[slot], at(a, b)))
    for copy in near_copies:
        copy.start()
    source = pairs[1:2, :]
    place = source >> 7
    slot = ((place >> 4) - row + 1) * 3 + ((place & 15) - col + 1)
    slot = jnp.where(slot == 4, 8, jnp.where(slot > 4, slot - 1, slot))
    for t in range(4):
        cut = slice(128 * t, 128 * t + 128)
        slots[t, 0:1] = slot[:, cut]
        slots[t, 1:2] = (source & 127)[:, cut]

    def second(k, _):
        drained(r1.at[k, pl.ds(0, N - 1)], r1_sem.at[k])

        @pl.when(k == 0)
        def _():
            drained(hr1, h_sem.at[1])

        lines = []
        for j in range(2):
            both = jnp.concatenate(
                [r1[k, :, j].reshape(N * TALL, 128), hr1[...].reshape(N * TALL, 128)], axis=1
            )
            lines.append(dot(both, into[2 * k + j]).astype(BF16))
        lines = jnp.concatenate(lines, axis=1)
        out = dot(yfwd[0], lines) + dot(yfwd[1], lines)
        for j in range(2):
            sb2[k, :, j] = out[:, 128 * j : 128 * j + 128].astype(BF16).reshape(N, 32, 128)
        exchange(sb2.at[k], r2.at[k], row, s2_sem.at[k], r2_sem.at[k], "row")
        return 0

    lax.fori_loop(0, CH, second, 0)
    for copy in k_copies:
        copy.wait()
    for copy in near_copies:
        copy.wait()
    n_copy.wait()

    def near_part(t):
        slot_rows = column(slots[t, 0:1]).astype(I32)
        place_rows = column(slots[t, 1:2]).astype(I32)
        lane = iota((LANES, LANES), 1)
        picked = jnp.zeros((LANES, LANES), F32)
        for s in range(9):
            table = qd[...] if s == 8 else nb[s]
            picked += dot(one_hot((slot_rows == s) & (place_rows == lane)), table)
        terms[t] = block_sums(nv, pl.multiple_of(128 * t, 128), picked, group)

    def first(k, _):
        near_part(2 * k)
        near_part(2 * k + 1)
        drained(r2.at[k, pl.ds(0, N - 1)], r2_sem.at[k])
        for j in range(2):
            sides = []
            for h in range(2):
                parts = [r2[k, 8 * h + q, j].astype(F32) for q in range(8)]
                sides.append(jnp.concatenate(transposed_groups(parts, lanes), axis=0).astype(BF16))
            lines = jnp.concatenate(sides, axis=1)
            spec = sum(dot(lines, ybwd[n, :, 0:16].reshape(G, P_SIZE)) for n in range(2))
            cols = []
            for h in range(4):
                weights = jnp.concatenate(
                    [kv[h, pl.ds(16 * k + 8 * j + q, 32, stride=32), :] for q in range(8)], axis=0
                )
                cols.append((spec[:, 128 * h : 128 * h + 128] * weights).astype(BF16))
            weighted = jnp.concatenate(cols, axis=1)
            field = dot(weighted, bwd[0]) + dot(weighted, bwd[1])
            for h in range(2):
                parts = [field[32 * q : 32 * q + 32, 128 * h : 128 * h + 128] for q in range(8)]
                for q, part in enumerate(transposed_groups(parts, lanes)):
                    sb3[k, 8 * h + q, j] = part.astype(BF16)
        exchange(sb3.at[k], r3.at[k], row, s3_sem.at[k], r3_sem.at[k], "row")
        return 0

    lax.fori_loop(0, CH, first, 0)
    near = jnp.zeros((LANES, LANES), F32)
    for t in range(4):
        target = pairs[0:1, 128 * t : 128 * t + 128] - 128 * (row * N + col)
        hot = one_hot(iota((LANES, LANES), 0) == target)
        for part in halves(terms[t]):
            near += dot(hot, part)
    terms[0] = near
    inverse[...] = jnp.zeros_like(inverse)

    def inverted(k, total):
        lines = order[pl.ds(pl.multiple_of(8 * k, 8), 8), :]
        for j in range(8):
            line = lines[j : j + 1, :]
            at_row = iota((ROWS, LANES), 0) == (line >> 7)
            both = jnp.concatenate(
                [
                    jnp.where(at_row, iota((ROWS, LANES), 1).astype(F32), 0.0),
                    jnp.where(at_row, (8 * k + j).astype(F32), 0.0),
                ],
                axis=0,
            ).astype(BF16)
            hot = one_hot(iota((LANES, LANES), 0) == (line & 127))
            total += lax.dot_general(
                both, hot, (((1,), (1,)), ((), ())), preferred_element_type=F32
            )
        return total

    acc[...] = jnp.zeros_like(acc)

    def second_back(k, _):
        def prepare(n, _):
            inverse[...] += inverted(4 * k + n, jnp.zeros((LANES, LANES), F32))
            return 0

        lax.fori_loop(0, 4, prepare, 0)
        drained(r3.at[k, pl.ds(0, N - 1)], r3_sem.at[k])
        lines = jnp.concatenate([r3[k, :, j].reshape(512, 128) for j in range(2)], axis=1)
        part = sum(dot(ybwd[n].reshape(N * TALL, P_SIZE), lines) for n in range(2)).astype(BF16)
        for j in range(2):
            moved = dot(part[:, 128 * j : 128 * j + 128], back[2 * k + j])
            sb4[k, :, j] = moved[:, 0:128].astype(BF16).reshape(N, TALL, 128)
            acc[...] += moved[:, 128:256]
        exchange(sb4.at[k], r4.at[k], col, s4_sem.at[k], r4_sem.at[k], "col")
        return 0

    lax.fori_loop(0, CH, second_back, 0)
    hs4[...] = acc[...].astype(BF16).reshape(N, TALL, 128)
    exchange_beside(hs4, hr4, h_sem.at[2], h_sem.at[3], -1)
    for k in range(CH):
        drained(sb1.at[k, pl.ds(0, N - 1)], s1_sem.at[k])
        drained(sb2.at[k, pl.ds(0, N - 1)], s2_sem.at[k])
        drained(sb3.at[k, pl.ds(0, N - 1)], s3_sem.at[k])
        drained(r4.at[k, pl.ds(0, N - 1)], r4_sem.at[k])
    drained(hs1, h_sem.at[0])
    drained(hr4, h_sem.at[3])
    for k in range(4):
        cols = slice(128 * k, 128 * k + 128)
        parts = [r4[q % 4 // 2, 4 * k + q // 4, q % 2].astype(F32) for q in range(16)]
        for q, part in enumerate(transposed_groups(parts, lanes)):
            s1[q, :, cols] = part
        parts = [hr4[4 * k + q].astype(F32) for q in range(4)]
        for q, part in enumerate(transposed_groups(parts, lanes)):
            s1[16 + q, :, cols] = part
    lines = s1[...].reshape(EXT, 512).astype(BF16)
    lines = jnp.concatenate([lines, jnp.zeros((PICK - EXT, 512), BF16)], axis=0)
    field = sum(
        lax.dot_general(zline[n], lines, (((1,), (1,)), ((), ())), preferred_element_type=F32)
        for n in range(2)
    )
    spot = cells[...]
    side, spot = spot >> 7, spot & 127
    lane = iota((LANES, LANES), 1)
    values = jnp.zeros((LANES, LANES), F32)
    for l in range(4):
        rows = field[128 * l : 128 * l + 128]
        value = looked_up(rows[:, 0:128], spot)
        for h in range(1, 4):
            value = jnp.where(side == h, looked_up(rows[:, 128 * h : 128 * h + 128], spot), value)
        values = jnp.where((lane & 3) == l, value, values)
    values = jnp.where(lane < BLK, values, 0.0).astype(BF16).astype(F32)
    values = values + pltpu.roll(values, BLK, 1)
    for k in range(CH):
        drained(sb4.at[k, pl.ds(0, N - 1)], s4_sem.at[k])
    drained(hs4, h_sem.at[2])
    i_copy.wait()

    total = block_sums(iv, 0, values, group) + terms[0]
    total = jnp.where(odd == right, total, 0.0)
    gather_rows = one_hot(iota((ROWS, LANES), 0) == (iota((ROWS, LANES), 1) >> 1))
    by_slot = sum(dot(gather_rows, part) for part in halves(total))
    back_order = inverse[...].astype(I32)
    out_ref[...] = permuted(by_slot, back_order[ROWS:] * 128 + back_order[:ROWS])


def solve(charges, order, anchor, pairs, project, interpolate, near_blocks, kernel_spectrum):
    consts = tables()
    vmem = pl.BlockSpec(memory_space=pltpu.VMEM)
    hbm = pl.BlockSpec(memory_space=pl.ANY)
    dma = pltpu.SemaphoreType.DMA
    return pl.pallas_call(
        solve_kernel,
        out_shape=jax.ShapeDtypeStruct((ROWS, LANES), F32),
        in_specs=[hbm] * 13,
        out_specs=vmem,
        scratch_shapes=[
            pltpu.VMEM((ROWS, LANES), BF16),
            pltpu.VMEM((ROWS, LANES), I32),
            pltpu.VMEM((3, LANES), I32),
            pltpu.VMEM((2, 512), I32),
            pltpu.VMEM((2, 512, 256), BF16),
            pltpu.VMEM((2, 512, N * TALL), BF16),
            pltpu.VMEM((2, N, TALL, 512), BF16),
            pltpu.VMEM((4, 256, 128), BF16),
            pltpu.VMEM((4, 128, 256), BF16),
            pltpu.VMEM((4096, LANES), BF16),
            pltpu.VMEM((2, 512, 512), BF16),
            pltpu.VMEM((128, 4096), BF16),
            pltpu.VMEM((128, 4096), BF16),
            pltpu.VMEM((512, 4096), BF16),
            pltpu.VMEM((LANES, LANES), BF16),
            pltpu.VMEM((LANES, LANES), I32),
            pltpu.VMEM((4, 8, LANES), I32),
            pltpu.VMEM((4, LANES, LANES), F32),
            pltpu.VMEM((LANES, LANES), F32),
            pltpu.VMEM((4, 1024, 128), F32),
            pltpu.VMEM((WIDE, TALL, 512), F32),
            pltpu.VMEM((CH, N, 2, TALL, 128), BF16),
            pltpu.VMEM((CH, N, 2, TALL, 128), BF16),
            pltpu.VMEM((N, TALL, 128), BF16),
            pltpu.VMEM((N, TALL, 128), BF16),
            pltpu.VMEM((CH, N, 2, 32, 128), BF16),
            pltpu.VMEM((CH, N, 2, 32, 128), BF16),
            pltpu.VMEM((CH, N, 2, 32, 128), BF16),
            pltpu.VMEM((CH, N, 2, 32, 128), BF16),
            pltpu.VMEM((CH, N, 2, TALL, 128), BF16),
            pltpu.VMEM((CH, N, 2, TALL, 128), BF16),
            pltpu.VMEM((N, TALL, 128), BF16),
            pltpu.VMEM((N, TALL, 128), BF16),
            pltpu.VMEM((N * TALL, 128), F32),
            pltpu.VMEM((8, LANES, LANES), BF16),
            dma((12,)),
            dma((4,)),
            dma((8,)),
            dma((8,)),
            dma((CH,)),
            dma((CH,)),
            dma((CH,)),
            dma((CH,)),
            dma((CH,)),
            dma((CH,)),
            dma((CH,)),
            dma((CH,)),
            dma((4,)),
        ],
        compiler_params=pltpu.CompilerParams(
            collective_id=0, has_side_effects=True, vmem_limit_bytes=62 << 20
        ),
    )(
        charges.reshape(ROWS, LANES),
        order.reshape(ROWS, LANES),
        anchor,
        pairs,
        project,
        interpolate,
        near_blocks,
        kernel_spectrum.reshape(1024, P_SIZE),
        *[jnp.asarray(part) for part in consts],
    )


def body(
    charges,
    panel_order,
    patch_anchor,
    project,
    interpolate,
    kernel_spectrum,
    near_pairs,
    near_blocks,
):
    out = solve(
        charges, panel_order, patch_anchor, near_pairs, project, interpolate, near_blocks,
        kernel_spectrum,
    )
    return out.reshape(ROWS * LANES)


def solution(mesh):
    placed = (
        P(("row", "col")),
        P(("row", "col")),
        P(None, ("row", "col")),
        P(("row", "col"), None),
        P(("row", "col"), None),
        P("row", "col", None),
        P(None, ("row", "col")),
        P(("row", "col"), None),
    )
    return jax.shard_map(
        body, mesh=mesh, in_specs=placed, out_specs=P(("row", "col")), check_vma=False
    )
```

time: 69.5 us -> 60.5 us (0.87)
  Pallas kernels: 68 us -> 58.9 us
    pallas_call x1, Pallas kernels: 68 us -> 58.9 us  [solve(): pl.pallas_call(solve_kernel, out_shape=jax.ShapeDtypeStruct((ROWS, LANES)...]
where the time goes in v2:
time: 60.5 us; the launch traced here: 60.3 us
  Pallas kernels  58.9 us (97%)
  local copies, waits for them, and re-layouts  1.38 us (2%)
    pallas_call x1, Pallas kernels, solve(): pl.pallas_call(solve_kernel, out_shape=jax.ShapeDtypeStruct((ROWS, LANES)...  58.9 us
    unnamed x1, local copies, waits for them, and re-layouts  1.38 us

profile of v2, /device:TPU:1, one launch (start us, length us, event | category | flops | bytes accessed | tf_op | source)
XLA Modules:
  0.0 60.3 jit_solution(8305272877026069379)
XLA Ops:
  0.0 58.9 %shard_map.127 = f32[64,128]{1,0:T(8,128)} custom-call(bf16[64,128]{1,0:T(8,128)(2,1)} %bitcast.7, s32[64,128]{1,0:T(8,128)} %bitcast.6, s32[3,128]{1,0:T(4,128)} %anchor_hbm.1, s32[2,512]{1,0:T(2,128)} %pairs_hbm.1, bf16[128,4096]{1,0:T(8,128)(2,1)} %project_hbm.1, bf16[128,4096]{1,0:T(8,128)(2,1)} %interp_hbm.1, bf16[512,4096]{1,0:T(8,128)(2,1)} %near_hbm.1, ...), custom_call_target="tpu_custom_call" | custom-call | tf_op jit(solution)/shard_map/pallas_call | solution.py:471
  58.9 1.4 %copy.15 = f32[8192]{0:T(1024)} copy(f32[8192]{0:T(1024)} %bitcast.5) | data formatting | bytes 65536

commit v3 on v2

--- a/solution.py
+++ b/solution.py
@@ -142,21 +142,6 @@
     def at(a, b):
         return (lax.rem(row + a + N, N), lax.rem(col + b + N, N))
 
-    barrier = pltpu.get_barrier_semaphore()
-
-    def greet(k, _):
-        pl.semaphore_signal(barrier, inc=1, device_id=at(k, 0), device_id_type=mesh_id)
-        pl.semaphore_signal(barrier, inc=1, device_id=at(0, k), device_id_type=mesh_id)
-        return 0
-
-    lax.fori_loop(1, N, greet, 0)
-
-    def greet_beside(k, _):
-        pl.semaphore_signal(barrier, inc=1, device_id=at(1, k), device_id_type=mesh_id)
-        pl.semaphore_signal(barrier, inc=1, device_id=at(-1, k), device_id_type=mesh_id)
-        return 0
-
-    lax.fori_loop(1, N, greet_beside, 0)
     small = [
         pltpu.make_async_copy(src, dst, in_sem.at[3 + n])
         for n, (src, dst) in enumerate(
@@ -175,15 +160,25 @@
     p_copy.start()
     for copy in small[4:]:
         copy.start()
+    barrier = pltpu.get_barrier_semaphore()
+
+    def greet(k, _):
+        pl.semaphore_signal(barrier, inc=1, device_id=at(k, 0), device_id_type=mesh_id)
+        pl.semaphore_signal(barrier, inc=1, device_id=at(0, k), device_id_type=mesh_id)
+        return 0
+
+    lax.fori_loop(1, N, greet, 0)
+
+    def greet_beside(k, _):
+        pl.semaphore_signal(barrier, inc=1, device_id=at(1, k), device_id_type=mesh_id)
+        pl.semaphore_signal(barrier, inc=1, device_id=at(-1, k), device_id_type=mesh_id)
+        return 0
+
+    lax.fori_loop(1, N, greet_beside, 0)
     k_copies = [
         pltpu.make_async_copy(k_hbm.at[:, pl.ds(128 * h, 128)], kv.at[h], k_sem.at[h])
         for h in range(4)
     ]
-    for copy in k_copies:
-        copy.start()
-    n_copy.start()
-    i_copy.start()
-
     def grouped(n, _):
         rows = pl.ds(pl.multiple_of(512 * n, 512), 512)
         group[rows] = one_hot(
@@ -206,6 +201,10 @@
     patch = block_sums(pv, 0, q_both, group)
     for copy in small[4:]:
         copy.wait()
+    for copy in k_copies:
+        copy.start()
+    n_copy.start()
+    i_copy.start()
     x_rows = column(anchor[0:1, :] - 16 * row).astype(I32)
     y_rows = column(anchor[1:2, :] - 16 * col).astype(I32)
     z_rows = column(anchor[2:3, :]).astype(I32)
@@ -246,7 +245,8 @@
         return lax.dot_general(a, b, (((0,), (0,)), ((), ())), preferred_element_type=F32)
 
     lanes = lax.broadcasted_iota(I32, (1, 128), 1)
-    spread = across(high, zline[0]) + across(high, zline[1]) + across(low, zline[0])
+    spread = across(high, jnp.concatenate([zline[0], zline[1]], axis=1))
+    spread = spread[:, 0:512] + spread[:, 512:1024] + across(low, zline[0])
     s1[...] = spread[0:EXT].reshape(WIDE, TALL, 512)
     for k in range(4):
         cols = slice(128 * k, 128 * k + 128)
@@ -287,8 +287,8 @@
 
         lax.fori_loop(0, N, one, 0)
 
+    exchange_beside(hs1, hr1, h_sem.at[0], h_sem.at[1], 1)
     exchange(sb1.at[0], r1.at[0], col, s1_sem.at[0], r1_sem.at[0], "col")
-    exchange_beside(hs1, hr1, h_sem.at[0], h_sem.at[1], 1)
     exchange(sb1.at[1], r1.at[1], col, s1_sem.at[1], r1_sem.at[1], "col")
     near_copies = []
     for k, (a, b) in enumerate(NEIGHBOURS):

time: 60.5 us -> 59.8 us (0.988)
    pallas_call x1, Pallas kernels: 58.9 us -> 58.3 us  [solve(): pl.pallas_call(solve_kernel, out_shape=jax.ShapeDtypeStruct((ROWS, LANES)...]
where the time goes in v3:
time: 59.8 us; the launch traced here: 59.6 us
  Pallas kernels  58.3 us (97%)
  local copies, waits for them, and re-layouts  1.38 us (2%)
    pallas_call x1, Pallas kernels, solve(): pl.pallas_call(solve_kernel, out_shape=jax.ShapeDtypeStruct((ROWS, LANES)...  58.3 us
    unnamed x1, local copies, waits for them, and re-layouts  1.38 us

profile of v3, /device:TPU:1, one launch (start us, length us, event | category | flops | bytes accessed | tf_op | source)
XLA Modules:
  0.0 59.6 jit_solution(17703220553940547883)
XLA Ops:
  0.0 58.3 %shard_map.127 = f32[64,128]{1,0:T(8,128)} custom-call(bf16[64,128]{1,0:T(8,128)(2,1)} %bitcast.7, s32[64,128]{1,0:T(8,128)} %bitcast.6, s32[3,128]{1,0:T(4,128)} %anchor_hbm.1, s32[2,512]{1,0:T(2,128)} %pairs_hbm.1, bf16[128,4096]{1,0:T(8,128)(2,1)} %project_hbm.1, bf16[128,4096]{1,0:T(8,128)(2,1)} %interp_hbm.1, bf16[512,4096]{1,0:T(8,128)(2,1)} %near_hbm.1, ...), custom_call_target="tpu_custom_call" | custom-call | tf_op jit(solution)/shard_map/pallas_call | solution.py:471
  58.3 1.4 %copy.15 = f32[8192]{0:T(1024)} copy(f32[8192]{0:T(1024)} %bitcast.5) | data formatting | bytes 65536

commit v4 on v3

--- a/solution.py
+++ b/solution.py
@@ -365,7 +365,16 @@
                 parts = [field[32 * q : 32 * q + 32, 128 * h : 128 * h + 128] for q in range(8)]
                 for q, part in enumerate(transposed_groups(parts, lanes)):
                     sb3[k, 8 * h + q, j] = part.astype(BF16)
-        exchange(sb3.at[k], r3.at[k], row, s3_sem.at[k], r3_sem.at[k], "row")
+
+            def send_half(n, _, j=j):
+                to = lax.rem(row + n, N)
+                remote(
+                    sb3.at[k, to, j], r3.at[k, row, j], s3_sem.at[k], r3_sem.at[k], (to, col)
+                ).start()
+                return 0
+
+            lax.fori_loop(1, N, send_half, 0)
+        r3[k, row] = sb3[k, row]
         return 0
 
     lax.fori_loop(0, CH, first, 0)

time: 59.8 us -> 60.8 us (1.017)
  Pallas kernels: 58.3 us -> 59.3 us
    pallas_call x1, Pallas kernels: 58.3 us -> 59.3 us  [solve(): pl.pallas_call(solve_kernel, out_shape=jax.ShapeDtypeStruct((ROWS, LANES)...]
where the time goes in v4:
time: 60.8 us; the launch traced here: 60.7 us
  Pallas kernels  59.3 us (98%)
  local copies, waits for them, and re-layouts  1.38 us (2%)
    pallas_call x1, Pallas kernels, solve(): pl.pallas_call(solve_kernel, out_shape=jax.ShapeDtypeStruct((ROWS, LANES)...  59.3 us
    unnamed x1, local copies, waits for them, and re-layouts  1.38 us

profile of v4, /device:TPU:1, one launch (start us, length us, event | category | flops | bytes accessed | tf_op | source)
XLA Modules:
  0.0 60.7 jit_solution(13504995522752509497)
XLA Ops:
  0.0 59.3 %shard_map.127 = f32[64,128]{1,0:T(8,128)} custom-call(bf16[64,128]{1,0:T(8,128)(2,1)} %bitcast.7, s32[64,128]{1,0:T(8,128)} %bitcast.6, s32[3,128]{1,0:T(4,128)} %anchor_hbm.1, s32[2,512]{1,0:T(2,128)} %pairs_hbm.1, bf16[128,4096]{1,0:T(8,128)(2,1)} %project_hbm.1, bf16[128,4096]{1,0:T(8,128)(2,1)} %interp_hbm.1, bf16[512,4096]{1,0:T(8,128)(2,1)} %near_hbm.1, ...), custom_call_target="tpu_custom_call" | custom-call | tf_op jit(solution)/shard_map/pallas_call | solution.py:480
  59.3 1.4 %copy.15 = f32[8192]{0:T(1024)} copy(f32[8192]{0:T(1024)} %bitcast.5) | data formatting | bytes 65536
